TPU v7x, 512 devices: a whole 4x4x16 slice. The times are simulated.
512 devices in a mesh: expert: 8 (over x, core), replica: 64 (over y, z).
Axes of the slice: x: 4, y: 4, z: 16, core: 2. Of those that a mesh axis runs over, the one named last changes fastest.
Arguments:
- pool: bfloat16 [64, 4096, 2048], P('replica', 'expert'), may hold values from -15 to 15
- row_index: int32 [8, 64, 256], P(None, 'replica'), may hold values from 0 to 4095, as said below
- counts: int32 [8, 64], P('expert', 'replica'), may hold values from 128 to 256, as said below
- targets: bfloat16 [8, 64, 256, 384], P('expert', 'replica'), may hold values from -4 to 4
- weights: float32 [8, 2, 2048, 384], P('expert', None, 'replica'), may hold values from -0.125 to 0.125
- first_moment: float32 [8, 2, 2048, 384], P('expert', None, 'replica'), may hold values from -1.5 to 1.5
- second_moment: float32 [8, 2, 2048, 384], P('expert', None, 'replica'), may hold values from 0.0001 to 0.01
Outputs:
- new_weights: float32 [8, 2, 2048, 384], P('expert', None, 'replica')
- new_first_moment: float32 [8, 2, 2048, 384], P('expert', None, 'replica')
- new_second_moment: float32 [8, 2, 2048, 384], P('expert', None, 'replica')
Inputs may be any that keep to these rules, and one draw needn't show every extreme that they name: `row_index`: for each expert and replica the 256 entries are distinct rows of that replica's 4096 tokens; at most 48 of them lie in any one aligned block of 512 rows, and some block holds exactly 48 of them. `counts`: at least 128 live slots for each expert on each replica; some expert on some replica has all 256 slots live.
All inputs are finite; a program needn't handle non-finite values.
Results may differ from a plain program's by a relative error of at most 0.0043.
Values may be sent and summed in bfloat16 or wider, within the bound.
A program may use at most 64 MiB of HBM per device.

v0:
```python
import jax
import jax.numpy as jnp
from jax import lax
from jax.sharding import Mesh
from jax.sharding import PartitionSpec as P

STEP = 3
EXPERT = ("expert_0", "expert_1")


beta_first = 0.9
beta_second = 0.999
learning_rate = 0.02
decay_rate = 0.1
adam_epsilon = 1e-08
adasum_epsilon = 1e-12


def cut_along(x, dim, devices):
    lengths = x.shape
    pieces = x.reshape(*lengths[:dim], devices, lengths[dim] // devices, *lengths[dim + 1 :])
    return jnp.moveaxis(pieces, dim, 0)


def laid_out(pieces, dim):
    lengths = list(pieces.shape[1:])
    lengths[dim] *= pieces.shape[0]
    return jnp.moveaxis(pieces, 0, dim).reshape(lengths)


def turned_blocks(pieces, axes, sequence):
    inside = pieces.shape[1:]
    whole = pieces.reshape(*(lax.axis_size(a) for a in axes), *inside)
    for k in sequence:
        whole = lax.all_to_all(whole, axes[k], k, k, tiled=True)
    return whole.reshape(-1, *inside)


def core_and_chips(x, groups, sequence, split_dim, concat_dim):
    devices = lax.axis_size(groups[0]) * lax.axis_size(groups[1])
    pieces = cut_along(x, split_dim, devices)
    return laid_out(turned_blocks(pieces, groups, sequence), concat_dim)


def from_everyone(x, axis):
    copies = jnp.broadcast_to(x, (lax.axis_size(axis), *x.shape))
    return lax.all_to_all(copies, axis, split_axis=0, concat_axis=0, tiled=True)


def of_everyone(x, axis):
    return from_everyone(x, axis).sum(axis=0)


def swapped(x, axis, bit):
    return lax.ppermute(x, axis, [(i, i ^ 1 << bit) for i in range(lax.axis_size(axis))])


def side_by_side(arrays, axis, dim, along):
    widths = [a.shape[along] for a in arrays]
    both = jnp.concatenate(arrays, axis=along)
    whole = lax.all_gather(both, axis, axis=dim, tiled=True)
    return tuple(jnp.split(whole, [sum(widths[:k]) for k in range(1, len(widths))], axis=along))


def row_contract(left_rows, right_rows):
    return lax.dot_general(
        left_rows, right_rows, (((0,), (0,)), ((), ())), preferred_element_type=jnp.float32
    )


def adam_update(gradient, weight, moment_one, moment_two):
    moment_one = beta_first * moment_one + (1.0 - beta_first) * gradient
    moment_two = beta_second * moment_two + (1.0 - beta_second) * gradient * gradient
    first_hat = moment_one / (1.0 - beta_first**STEP)
    second_hat = moment_two / (1.0 - beta_second**STEP)
    weight = weight - learning_rate * (
        first_hat / (jnp.sqrt(second_hat) + adam_epsilon) + decay_rate * weight
    )
    return (weight, moment_one, moment_two)


def fetch_rows(pool, row_index):
    experts = lax.axis_size(EXPERT)
    expert_position = lax.axis_index(EXPERT)
    local_pool = pool[0]
    shard_rows = local_pool.shape[0]
    listed = row_index[:, 0, :]
    capacity = listed.shape[1]
    per_source = 3 * capacity // (2 * experts)
    source_shard = listed // shard_rows
    shard_onehot = (source_shard[:, :, None] == lax.iota(jnp.int32, experts)[None, None, :]).astype(
        jnp.int32
    )
    earlier = jnp.cumsum(shard_onehot, axis=1) - shard_onehot
    slot_rank = jnp.sum(earlier * shard_onehot, axis=2)
    held_here = source_shard == expert_position
    target_slot = jnp.where(held_here, slot_rank, per_source)
    destination = jnp.broadcast_to(lax.iota(jnp.int32, experts)[:, None], listed.shape)
    send_table = (
        jnp.zeros((experts, per_source), jnp.int32)
        .at[destination, target_slot]
        .set(listed - expert_position * shard_rows, mode="drop")
    )
    outgoing = local_pool[send_table]
    incoming = core_and_chips(outgoing, ("expert_0", "expert_1"), (1, 0), 0, 0)
    own_shard = lax.dynamic_index_in_dim(source_shard, expert_position, 0, keepdims=False)
    own_rank = lax.dynamic_index_in_dim(slot_rank, expert_position, 0, keepdims=False)
    flat_incoming = incoming.reshape(experts * per_source, incoming.shape[2])
    return flat_incoming[own_shard * per_source + own_rank]


def group_totals(partial_sums, position, bit_number):
    slot_count = 1 << bit_number
    group_owner = position % slot_count
    onehot = (lax.iota(jnp.int32, slot_count) == group_owner).astype(jnp.float32)
    group_table = of_everyone(onehot[:, None] * partial_sums[None, :], "replica")
    return jnp.dot(onehot, group_table, precision=lax.Precision.HIGHEST)


def combine_level(own_half, other_half, upper_bit, position, bit_number):
    partial_list = []
    for own_matrix, other_matrix in zip(own_half, other_half):
        inner_product = jnp.sum(own_matrix * other_matrix)
        own_square = jnp.sum(own_matrix * own_matrix)
        other_square = jnp.sum(other_matrix * other_matrix)
        partial_list.append(inner_product)
        partial_list.append(jnp.where(upper_bit == 0, own_square, other_square))
        partial_list.append(jnp.where(upper_bit == 0, other_square, own_square))
    totals = group_totals(jnp.stack(partial_list), position, bit_number)
    merged = []
    for member in range(2):
        inner_product = totals[3 * member]
        first_weight = 1.0 - inner_product / (2.0 * totals[3 * member + 1] + adasum_epsilon)
        second_weight = 1.0 - inner_product / (2.0 * totals[3 * member + 2] + adasum_epsilon)
        own_weight = jnp.where(upper_bit == 0, first_weight, second_weight)
        other_weight = jnp.where(upper_bit == 0, second_weight, first_weight)
        merged.append(own_weight * own_half[member] + other_weight * other_half[member])
    return tuple(merged)


def swap_halves(matrices, upper_bit, bit_number):
    half_rows = matrices[0].shape[0] // 2
    kept_half = tuple(
        (
            lax.dynamic_slice_in_dim(matrix, upper_bit * half_rows, half_rows, 0)
            for matrix in matrices
        )
    )
    sent_half = tuple(
        (
            lax.dynamic_slice_in_dim(matrix, (1 - upper_bit) * half_rows, half_rows, 0)
            for matrix in matrices
        )
    )
    received = swapped((sent_half[0], sent_half[1]), "replica", bit_number)
    return (kept_half, received)


def shards(pool, row_index, counts, targets, weights, first_moment, second_moment):
    replicas = lax.axis_size("replica")
    levels = replicas.bit_length() - 1
    position = lax.axis_index("replica")
    inputs = fetch_rows(pool, row_index)
    live_count = counts[0, 0]
    capacity = inputs.shape[0]
    lowered = weights[0].astype(jnp.bfloat16)
    pieces = side_by_side((lowered[0], lowered[1]), "replica", 0, 1)
    gate_value = jnp.dot(inputs, pieces[0], preferred_element_type=jnp.float32)
    up_value = jnp.dot(inputs, pieces[1], preferred_element_type=jnp.float32)
    sigmoid = jax.nn.sigmoid(gate_value)
    activated = gate_value * sigmoid
    silu_slope = sigmoid * (1.0 + gate_value * (1.0 - sigmoid))
    live = (lax.iota(jnp.int32, capacity) < live_count).astype(jnp.float32)[:, None]
    residual = (
        (activated * up_value - targets[0, 0].astype(jnp.float32))
        * live
        / live_count.astype(jnp.float32)
    )
    gate_delta = (residual * up_value * silu_slope).astype(jnp.bfloat16)
    up_delta = (residual * activated).astype(jnp.bfloat16)
    bit_number = levels - 1
    upper_bit = position >> bit_number & 1
    half_columns = inputs.shape[1] // 2
    kept_columns = lax.dynamic_slice_in_dim(inputs, upper_bit * half_columns, half_columns, 1)
    sent_columns = lax.dynamic_slice_in_dim(inputs, (1 - upper_bit) * half_columns, half_columns, 1)
    partner_columns, partner_gate, partner_up = swapped(
        (sent_columns, gate_delta, up_delta), "replica", bit_number
    )
    own_half = (row_contract(kept_columns, gate_delta), row_contract(kept_columns, up_delta))
    other_half = (
        row_contract(partner_columns, partner_gate),
        row_contract(partner_columns, partner_up),
    )
    matrices = combine_level(own_half, other_half, upper_bit, position, bit_number)
    start_level = 1
    for level_number in range(start_level, levels):
        bit_number = levels - 1 - level_number
        upper_bit = position >> bit_number & 1
        own_half, other_half = swap_halves(matrices, upper_bit, bit_number)
        matrices = combine_level(own_half, other_half, upper_bit, position, bit_number)
    combined = jnp.stack(matrices)
    new_weight, moment_one, moment_two = adam_update(
        combined, weights[0], first_moment[0], second_moment[0]
    )
    return (new_weight[None], moment_one[None], moment_two[None])


def solution(mesh):
    split = Mesh(
        mesh.devices.reshape(4, 2, mesh.shape["replica"]), ("expert_0", "expert_1", "replica")
    )
    in_specs = (
        P("replica", EXPERT, None),
        P(None, "replica", None),
        P(EXPERT, "replica"),
        P(EXPERT, "replica", None, None),
        P(EXPERT, None, "replica", None),
        P(EXPERT, None, "replica", None),
        P(EXPERT, None, "replica", None),
    )
    out_specs = (
        P(EXPERT, None, "replica", None),
        P(EXPERT, None, "replica", None),
        P(EXPERT, None, "replica", None),
    )
    return jax.shard_map(
        shards, mesh=split, in_specs=in_specs, out_specs=out_specs, check_vma=False
    )
```

profile of v0, /device:TPU:4, one launch (start us, length us, event | category | flops | bytes accessed | tf_op | source)
XLA Modules:
  0.0 561.2 jit_solution(15794154442979309247)
XLA Ops:
  9.7 4.5 reduce-window.6
  17.7 8.0 %scatter_custom_fusion = s32[384]{0:T(512)S(1)} fusion(s32[2048]{0:T(1024)S(1)} %bitcast.176, s32[2048]{0:T(1024)S(1)} %bitcast.177, s32[]{:T(128)} %constant.196.clone.1), kind=kCustom, calls=%fused_computation.153 | custom fusion | bytes 1540
  25.9 3.1 gather_fusion
  29.0 1.5 copy.36
  30.5 5.0 all_to_all.40
  36.8 10.2 %all-to-all-start.1 = ((bf16[4,2,1,48,2048]{4,3,1,2,0:T(8,128)(2,1)}), bf16[4,2,1,48,2048]{4,3,1,2,0:T(8,128)(2,1)}, u32[]{:S(2)}, u32[]{:S(2)}) async-start(bf16[4,2,1,48,2048]{4,3,1,2,0:T(8,128)(2,1)} %copy.37), calls=%async_computation.1 | async-start | bytes 3145728 | tf_op jit(solution)/shard_map/all_to_all | solution.py:35
  47.7 17.7 %all-to-all-done.1 = bf16[4,2,1,48,2048]{4,3,1,2,0:T(8,128)(2,1)} async-done(((bf16[4,2,1,48,2048]{4,3,1,2,0:T(8,128)(2,1)}), bf16[4,2,1,48,2048]{4,3,1,2,0:T(8,128)(2,1)}, u32[]{:S(2)}, u32[]{:S(2)}) %all-to-all-start.1) | async-done | bytes 1572896 | tf_op jit(solution)/shard_map/all_to_all | solution.py:35
  65.4 4.0 gather_fusion.1
  70.2 2.0 collective-permute-start
  72.3 87.1 %all-gather.2.cloned.1.call-done = bf16[2048,768]{1,0:T(8,128)(2,1)} async-done(((bf16[32,768]{1,0:T(8,128)(2,1)}), bf16[2048,768]{1,0:T(8,128)(2,1)}) %all-gather.2.cloned.1.call-update) | async-done | bytes 3145744 | tf_op jit(solution)/shard_map/all_gather | solution.py:61
  159.3 2.3 fusion
  162.6 3.3 collective-permute-start.2
  165.9 4.1 collective-permute-start.1
  170.4 1.6 fusion.6
  172.1 3.3 multiply_reduce_fusion
  177.9 3.9 multiply_reduce_fusion.3
  186.6 9.4 %all-to-all-start.2 = ((f32[64,1,192]{2,1,0:T(1,128)}), f32[64,1,192]{2,1,0:T(1,128)S(1)}, u32[]{:S(2)}, u32[]{:S(2)}) async-start(f32[64,1,192]{2,1,0:T(1,128)} %reshape.548), calls=%async_computation.2 | async-start | bytes 131072 | tf_op jit(solution)/shard_map/all_to_all | solution.py:47
  196.0 14.7 %all-to-all-done.2 = f32[64,1,192]{2,1,0:T(1,128)S(1)} async-done(((f32[64,1,192]{2,1,0:T(1,128)}), f32[64,1,192]{2,1,0:T(1,128)S(1)}, u32[]{:S(2)}, u32[]{:S(2)}) %all-to-all-start.2) | async-done | bytes 49184 | tf_op jit(solution)/shard_map/all_to_all | solution.py:47
  218.0 2.2 multiply_add_fusion.1
  221.2 2.7 collective-permute-start.3
  225.5 3.4 collective-permute-start.4
  229.0 10.5 %collective-permute-done.3 = f32[512,384]{1,0:T(8,128)S(1)} collective-permute-done((f32[512,384]{1,0:T(8,128)}, f32[512,384]{1,0:T(8,128)S(1)}, u32[]{:S(2)}, u32[]{:S(2)}) %collective-permute-start.3) | collective-permute-done | bytes 786464 | tf_op jit(solution)/shard_map/ppermute | solution.py:55
  239.5 8.5 %collective-permute-done.4 = f32[512,384]{1,0:T(8,128)} collective-permute-done((f32[512,384]{1,0:T(8,128)}, f32[512,384]{1,0:T(8,128)}, u32[]{:S(2)}, u32[]{:S(2)}) %collective-permute-start.4) | collective-permute-done | bytes 786464 | tf_op jit(solution)/shard_map/ppermute | solution.py:55
  248.0 2.6 multiply_reduce_fusion.7
  257.8 4.6 all-to-all-start.3
  262.4 16.6 %all-to-all-done.3 = f32[64,16,6]{1,2,0:T(8,128)S(1)} async-done(((f32[64,16,6]{1,2,0:T(8,128)}), f32[64,16,6]{1,2,0:T(8,128)S(1)}, u32[]{:S(2)}, u32[]{:S(2)}) %all-to-all-start.3) | async-done | bytes 24608 | tf_op jit(solution)/shard_map/all_to_all | solution.py:47
  284.9 1.6 multiply_add_fusion.2
  287.4 5.4 collective-permute-start.6
  294.6 9.1 %collective-permute-start.5 = (f32[256,384]{1,0:T(8,128)}, f32[256,384]{1,0:T(8,128)}, u32[]{:S(2)}, u32[]{:S(2)}) collective-permute-start(f32[256,384]{1,0:T(8,128)} %constant_dynamic-slice_fusion.7), channel_id=1, source_target_pairs={{0,8},{1,9},{2,10},{3,11},{4,12},{5,13},{6,14},{7,15},{8,0},{9,1},... | collective-permute-start | bytes 1179656 | tf_op jit(solution)/shard_map/ppermute | solution.py:55
  303.7 16.7 %collective-permute-done.6 = f32[256,384]{1,0:T(8,128)S(1)} collective-permute-done((f32[256,384]{1,0:T(8,128)}, f32[256,384]{1,0:T(8,128)S(1)}, u32[]{:S(2)}, u32[]{:S(2)}) %collective-permute-start.6) | collective-permute-done | bytes 393248 | tf_op jit(solution)/shard_map/ppermute | solution.py:55
  323.7 10.3 %collective-permute-done.5 = f32[256,384]{1,0:T(8,128)} collective-permute-done((f32[256,384]{1,0:T(8,128)}, f32[256,384]{1,0:T(8,128)}, u32[]{:S(2)}, u32[]{:S(2)}) %collective-permute-start.5) | collective-permute-done | bytes 393248 | tf_op jit(solution)/shard_map/ppermute | solution.py:55
  334.0 1.8 multiply_reduce_fusion.16
  340.6 28.8 %all-to-all-start.4 = ((f32[64,8,6]{1,2,0:T(8,128)}), f32[64,8,6]{1,2,0:T(8,128)S(1)}, u32[]{:S(2)}, u32[]{:S(2)}) async-start(f32[64,8,6]{1,2,0:T(8,128)} %broadcast_in_dim.25), calls=%async_computation.4 | async-start | bytes 524288 | tf_op jit(solution)/shard_map/all_to_all | solution.py:47
  369.5 17.9 %all-to-all-done.4 = f32[64,8,6]{1,2,0:T(8,128)S(1)} async-done(((f32[64,8,6]{1,2,0:T(8,128)}), f32[64,8,6]{1,2,0:T(8,128)S(1)}, u32[]{:S(2)}, u32[]{:S(2)}) %all-to-all-start.4) | async-done | bytes 12320 | tf_op jit(solution)/shard_map/all_to_all | solution.py:47
  394.6 3.9 collective-permute-start.8
  399.6 5.9 %collective-permute-start.7 = (f32[128,384]{1,0:T(8,128)S(1)}, f32[128,384]{1,0:T(8,128)S(1)}, u32[]{:S(2)}, u32[]{:S(2)}) collective-permute-start(f32[128,384]{1,0:T(8,128)S(1)} %constant_dynamic-slice_fusion.5), channel_id=1, source_target_pairs={{0,4},{1,5},{2,6},{3,7},{4,0},{5,1},{6,2},{7,3},{8,12},{9,13},{10,... | collective-permute-start | bytes 589832 | tf_op jit(solution)/shard_map/ppermute | solution.py:55
  405.5 22.8 %collective-permute-done.8 = f32[128,384]{1,0:T(8,128)S(1)} collective-permute-done((f32[128,384]{1,0:T(8,128)S(1)}, f32[128,384]{1,0:T(8,128)S(1)}, u32[]{:S(2)}, u32[]{:S(2)}) %collective-permute-start.8) | collective-permute-done | bytes 196640 | tf_op jit(solution)/shard_map/ppermute | solution.py:55
  437.1 8.1 %all-to-all-start.5 = ((f32[64,4,6]{2,1,0:T(4,128)}), f32[64,4,6]{2,1,0:T(4,128)S(1)}, u32[]{:S(2)}, u32[]{:S(2)}) async-start(f32[64,4,6]{2,1,0:T(4,128)} %broadcast_in_dim.26), calls=%async_computation.5 | async-start | bytes 262144 | tf_op jit(solution)/shard_map/all_to_all | solution.py:47
  445.2 16.2 %all-to-all-done.5 = f32[64,4,6]{2,1,0:T(4,128)S(1)} async-done(((f32[64,4,6]{2,1,0:T(4,128)}), f32[64,4,6]{2,1,0:T(4,128)S(1)}, u32[]{:S(2)}, u32[]{:S(2)}) %all-to-all-start.5) | async-done | bytes 6176 | tf_op jit(solution)/shard_map/all_to_all | solution.py:47
  467.6 3.5 collective-permute-start.10
  471.1 3.4 collective-permute-start.9
  474.5 3.2 collective-permute-done.10
  486.2 7.0 %all-to-all-start.6 = ((f32[64,2,6]{2,1,0:T(2,128)}), f32[64,2,6]{2,1,0:T(2,128)S(1)}, u32[]{:S(2)}, u32[]{:S(2)}) async-start(f32[64,2,6]{2,1,0:T(2,128)} %broadcast_in_dim.27), calls=%async_computation.6 | async-start | bytes 131072 | tf_op jit(solution)/shard_map/all_to_all | solution.py:47
  493.2 14.7 %all-to-all-done.6 = f32[64,2,6]{2,1,0:T(2,128)S(1)} async-done(((f32[64,2,6]{2,1,0:T(2,128)}), f32[64,2,6]{2,1,0:T(2,128)S(1)}, u32[]{:S(2)}, u32[]{:S(2)}) %all-to-all-start.6) | async-done | bytes 3104 | tf_op jit(solution)/shard_map/all_to_all | solution.py:47
  514.1 2.6 collective-permute-start.12
  516.7 3.2 collective-permute-start.11
  527.8 18.9 %all_to_all.41 = f32[64,1,6]{2,1,0:T(1,128)S(1)} all-to-all(f32[64,1,6]{2,1,0:T(1,128)S(1)} %broadcast_in_dim.28), channel_id=1, replica_groups=mesh['expert_0'=4,'expert_1'=2,'replica'=64] {'replica'}, dimensions={0} | all-to-all | bytes 3072 | tf_op jit(solution)/shard_map/all_to_all | solution.py:47
  552.7 1.6 multiply_subtract_fusion
  (141 shorter events, 40.7 us)
Async XLA Ops:
  7.2 18.7 %copy-start = (bf16[1,512,2048]{2,1,0:T(8,128)(2,1)S(1)}, bf16[1,512,2048]{2,1,0:T(8,128)(2,1)}, u32[]{:S(2)}) copy-start(bf16[1,512,2048]{2,1,0:T(8,128)(2,1)} %param.7) | copy-start | bytes 6291460
  7.2 152.1 %all-gather.2.cloned.1.call-start = ((), (), s32[]{:S(2)}) async-start(), calls=%async_computation.8 | async-start | bytes 3194880 | tf_op jit(solution)/shard_map/all_gather | solution.py:61
  36.8 28.6 %all-to-all-start.1 = ((bf16[4,2,1,48,2048]{4,3,1,2,0:T(8,128)(2,1)}), bf16[4,2,1,48,2048]{4,3,1,2,0:T(8,128)(2,1)}, u32[]{:S(2)}, u32[]{:S(2)}) async-start(bf16[4,2,1,48,2048]{4,3,1,2,0:T(8,128)(2,1)} %copy.37), calls=%async_computation.1 | async-start | bytes 3145728 | tf_op jit(solution)/shard_map/all_to_all | solution.py:35
  70.2 91.4 %copy-start.15 = (bf16[1,1,256,384]{3,2,1,0:T(8,128)(2,1)S(1)}, bf16[1,1,256,384]{3,2,1,0:T(8,128)(2,1)}, u32[]{:S(2)}) copy-start(bf16[1,1,256,384]{3,2,1,0:T(8,128)(2,1)} %param.10) | copy-start | bytes 589828
  70.2 101.9 %collective-permute-start = (bf16[256,1024]{1,0:T(8,128)(2,1)}, bf16[256,1024]{1,0:T(8,128)(2,1)}, u32[]{:S(2)}, u32[]{:S(2)}) collective-permute-start(bf16[256,1024]{1,0:T(8,128)(2,1)} %constant_dynamic-slice_fusion.10), channel_id=1, source_target_pairs={{0,32},{1,33},{2,34},{3,35},{4,36},{5,37},{6,38},{7,39},{8,40},{9,... | collective-permute-start | bytes 1572872 | tf_op jit(solution)/shard_map/ppermute | solution.py:55
  159.3 2.4 copy-start.14
  162.6 9.5 %collective-permute-start.2 = (bf16[256,384]{1,0:T(8,128)(2,1)S(1)}, bf16[256,384]{1,0:T(8,128)(2,1)S(1)}, u32[]{:S(2)}, u32[]{:S(2)}) collective-permute-start(bf16[256,384]{1,0:T(8,128)(2,1)S(1)} %get-tuple-element.43), channel_id=1, source_target_pairs={{0,32},{1,33},{2,34},{3,35},{4,36},{5,37},{6,38},{7,39},{8,40},{9,... | collective-permute-start | bytes 589832 | tf_op jit(solution)/shard_map/ppermute | solution.py:55
  165.9 12.1 %collective-permute-start.1 = (bf16[256,384]{1,0:T(8,128)(2,1)S(1)}, bf16[256,384]{1,0:T(8,128)(2,1)S(1)}, u32[]{:S(2)}, u32[]{:S(2)}) collective-permute-start(bf16[256,384]{1,0:T(8,128)(2,1)S(1)} %get-tuple-element.42), channel_id=1, source_target_pairs={{0,32},{1,33},{2,34},{3,35},{4,36},{5,37},{6,38},{7,39},{8,40},{9,... | collective-permute-start | bytes 589832 | tf_op jit(solution)/shard_map/ppermute | solution.py:55
  170.4 4.9 copy-start.1
  186.6 24.1 %all-to-all-start.2 = ((f32[64,1,192]{2,1,0:T(1,128)}), f32[64,1,192]{2,1,0:T(1,128)S(1)}, u32[]{:S(2)}, u32[]{:S(2)}) async-start(f32[64,1,192]{2,1,0:T(1,128)} %reshape.548), calls=%async_computation.2 | async-start | bytes 131072 | tf_op jit(solution)/shard_map/all_to_all | solution.py:47
  218.0 5.9 %copy-start.6 = (f32[1024,384]{1,0:T(8,128)S(1)}, f32[1024,384]{1,0:T(8,128)}, u32[]{:S(2)}) copy-start(f32[1024,384]{1,0:T(8,128)} %get-tuple-element.85) | copy-start | bytes 4718596
  220.2 3.9 copy-start.3
  220.2 3.7 copy-start.2
  221.2 18.3 %collective-permute-start.3 = (f32[512,384]{1,0:T(8,128)}, f32[512,384]{1,0:T(8,128)S(1)}, u32[]{:S(2)}, u32[]{:S(2)}) collective-permute-start(f32[512,384]{1,0:T(8,128)} %constant_dynamic-slice_fusion.9), channel_id=1, source_target_pairs={{0,16},{1,17},{2,18},{3,19},{4,20},{5,21},{6,22},{7,23},{8,24},{9,... | collective-permute-start | bytes 2359304 | tf_op jit(solution)/shard_map/ppermute | solution.py:55
  224.1 1.4 copy-start.5
  225.5 22.5 %collective-permute-start.4 = (f32[512,384]{1,0:T(8,128)}, f32[512,384]{1,0:T(8,128)}, u32[]{:S(2)}, u32[]{:S(2)}) collective-permute-start(f32[512,384]{1,0:T(8,128)} %constant_dynamic-slice_fusion.8), channel_id=1, source_target_pairs={{0,16},{1,17},{2,18},{3,19},{4,20},{5,21},{6,22},{7,23},{8,24},{9,... | collective-permute-start | bytes 2359304 | tf_op jit(solution)/shard_map/ppermute | solution.py:55
  239.5 11.1 %copy-start.9 = (f32[512,384]{1,0:T(8,128)}, f32[512,384]{1,0:T(8,128)S(1)}, u32[]{:S(2)}) copy-start(f32[512,384]{1,0:T(8,128)S(1)} %collective-permute-done.3) | copy-start | bytes 2359300
  257.8 21.2 %all-to-all-start.3 = ((f32[64,16,6]{1,2,0:T(8,128)}), f32[64,16,6]{1,2,0:T(8,128)S(1)}, u32[]{:S(2)}, u32[]{:S(2)}) async-start(f32[64,16,6]{1,2,0:T(8,128)} %broadcast_in_dim.24), calls=%async_computation.3 | async-start | bytes 524288 | tf_op jit(solution)/shard_map/all_to_all | solution.py:47
  284.9 7.9 %copy-start.4 = (f32[1024,384]{1,0:T(8,128)S(1)}, f32[1024,384]{1,0:T(8,128)}, u32[]{:S(2)}) copy-start(f32[1024,384]{1,0:T(8,128)} %copy-done.3) | copy-start | bytes 4718596
  284.9 7.9 %copy-start.10 = (f32[512,384]{1,0:T(8,128)S(1)}, f32[512,384]{1,0:T(8,128)}, u32[]{:S(2)}) copy-start(f32[512,384]{1,0:T(8,128)} %copy-done.9) | copy-start | bytes 2359300
  287.4 33.0 %collective-permute-start.6 = (f32[256,384]{1,0:T(8,128)}, f32[256,384]{1,0:T(8,128)S(1)}, u32[]{:S(2)}, u32[]{:S(2)}) collective-permute-start(f32[256,384]{1,0:T(8,128)} %constant_dynamic-slice_fusion.6), channel_id=1, source_target_pairs={{0,8},{1,9},{2,10},{3,11},{4,12},{5,13},{6,14},{7,15},{8,0},{9,1},... | collective-permute-start | bytes 1179656 | tf_op jit(solution)/shard_map/ppermute | solution.py:55
  292.9 0.9 copy-start.7
  294.6 39.5 %collective-permute-start.5 = (f32[256,384]{1,0:T(8,128)}, f32[256,384]{1,0:T(8,128)}, u32[]{:S(2)}, u32[]{:S(2)}) collective-permute-start(f32[256,384]{1,0:T(8,128)} %constant_dynamic-slice_fusion.7), channel_id=1, source_target_pairs={{0,8},{1,9},{2,10},{3,11},{4,12},{5,13},{6,14},{7,15},{8,0},{9,1},... | collective-permute-start | bytes 1179656 | tf_op jit(solution)/shard_map/ppermute | solution.py:55
  320.4 73.0 %copy-start.11 = (f32[256,384]{1,0:T(8,128)}, f32[256,384]{1,0:T(8,128)S(1)}, u32[]{:S(2)}) copy-start(f32[256,384]{1,0:T(8,128)S(1)} %collective-permute-done.6) | copy-start | bytes 1179652
  340.6 46.8 %all-to-all-start.4 = ((f32[64,8,6]{1,2,0:T(8,128)}), f32[64,8,6]{1,2,0:T(8,128)S(1)}, u32[]{:S(2)}, u32[]{:S(2)}) async-start(f32[64,8,6]{1,2,0:T(8,128)} %broadcast_in_dim.25), calls=%async_computation.4 | async-start | bytes 524288 | tf_op jit(solution)/shard_map/all_to_all | solution.py:47
  393.4 5.1 copy-start.8
  394.6 33.7 %collective-permute-start.8 = (f32[128,384]{1,0:T(8,128)S(1)}, f32[128,384]{1,0:T(8,128)S(1)}, u32[]{:S(2)}, u32[]{:S(2)}) collective-permute-start(f32[128,384]{1,0:T(8,128)S(1)} %constant_dynamic-slice_fusion.4), channel_id=1, source_target_pairs={{0,4},{1,5},{2,6},{3,7},{4,0},{5,1},{6,2},{7,3},{8,12},{9,13},{10,... | collective-permute-start | bytes 589832 | tf_op jit(solution)/shard_map/ppermute | solution.py:55
  399.6 32.2 %collective-permute-start.7 = (f32[128,384]{1,0:T(8,128)S(1)}, f32[128,384]{1,0:T(8,128)S(1)}, u32[]{:S(2)}, u32[]{:S(2)}) collective-permute-start(f32[128,384]{1,0:T(8,128)S(1)} %constant_dynamic-slice_fusion.5), channel_id=1, source_target_pairs={{0,4},{1,5},{2,6},{3,7},{4,0},{5,1},{6,2},{7,3},{8,12},{9,13},{10,... | collective-permute-start | bytes 589832 | tf_op jit(solution)/shard_map/ppermute | solution.py:55
  437.1 24.3 %all-to-all-start.5 = ((f32[64,4,6]{2,1,0:T(4,128)}), f32[64,4,6]{2,1,0:T(4,128)S(1)}, u32[]{:S(2)}, u32[]{:S(2)}) async-start(f32[64,4,6]{2,1,0:T(4,128)} %broadcast_in_dim.26), calls=%async_computation.5 | async-start | bytes 262144 | tf_op jit(solution)/shard_map/all_to_all | solution.py:47
  467.6 85.1 %copy-start.12 = (f32[1,2,32,384]{3,2,1,0:T(8,128)S(1)}, f32[1,2,32,384]{3,2,1,0:T(8,128)}, u32[]{:S(2)}) copy-start(f32[1,2,32,384]{3,2,1,0:T(8,128)} %param.11) | copy-start | bytes 294916
  467.6 85.1 %copy-start.13 = (f32[1,2,32,384]{3,2,1,0:T(8,128)S(1)}, f32[1,2,32,384]{3,2,1,0:T(8,128)}, u32[]{:S(2)}) copy-start(f32[1,2,32,384]{3,2,1,0:T(8,128)} %param.12) | copy-start | bytes 294916
  467.6 10.2 %collective-permute-start.10 = (f32[64,384]{1,0:T(8,128)S(1)}, f32[64,384]{1,0:T(8,128)S(1)}, u32[]{:S(2)}, u32[]{:S(2)}) collective-permute-start(f32[64,384]{1,0:T(8,128)S(1)} %constant_dynamic-slice_fusion.2), channel_id=1, source_target_pairs={{0,2},{1,3},{2,0},{3,1},{4,6},{5,7},{6,4},{7,5},{8,10},{9,11},{10,... | collective-permute-start | bytes 294920 | tf_op jit(solution)/shard_map/ppermute | solution.py:55
  471.1 9.9 %collective-permute-start.9 = (f32[64,384]{1,0:T(8,128)S(1)}, f32[64,384]{1,0:T(8,128)S(1)}, u32[]{:S(2)}, u32[]{:S(2)}) collective-permute-start(f32[64,384]{1,0:T(8,128)S(1)} %constant_dynamic-slice_fusion.3), channel_id=1, source_target_pairs={{0,2},{1,3},{2,0},{3,1},{4,6},{5,7},{6,4},{7,5},{8,10},{9,11},{10,... | collective-permute-start | bytes 294920 | tf_op jit(solution)/shard_map/ppermute | solution.py:55
  486.2 21.7 %all-to-all-start.6 = ((f32[64,2,6]{2,1,0:T(2,128)}), f32[64,2,6]{2,1,0:T(2,128)S(1)}, u32[]{:S(2)}, u32[]{:S(2)}) async-start(f32[64,2,6]{2,1,0:T(2,128)} %broadcast_in_dim.27), calls=%async_computation.6 | async-start | bytes 131072 | tf_op jit(solution)/shard_map/all_to_all | solution.py:47
  514.1 6.0 %collective-permute-start.12 = (f32[32,384]{1,0:T(8,128)S(1)}, f32[32,384]{1,0:T(8,128)S(1)}, u32[]{:S(2)}, u32[]{:S(2)}) collective-permute-start(f32[32,384]{1,0:T(8,128)S(1)} %constant_dynamic-slice_fusion), channel_id=1, source_target_pairs={{0,1},{1,0},{2,3},{3,2},{4,5},{5,4},{6,7},{7,6},{8,9},{9,8},{10,11... | collective-permute-start | bytes 147464 | tf_op jit(solution)/shard_map/ppermute | solution.py:55
  516.7 6.5 %collective-permute-start.11 = (f32[32,384]{1,0:T(8,128)S(1)}, f32[32,384]{1,0:T(8,128)S(1)}, u32[]{:S(2)}, u32[]{:S(2)}) collective-permute-start(f32[32,384]{1,0:T(8,128)S(1)} %constant_dynamic-slice_fusion.1), channel_id=1, source_target_pairs={{0,1},{1,0},{2,3},{3,2},{4,5},{5,4},{6,7},{7,6},{8,9},{9,8},{10,11... | collective-permute-start | bytes 147464 | tf_op jit(solution)/shard_map/ppermute | solution.py:55
Sparse Core Ops, SparseCore 0:
  11.5 147.7 all-gather.1
where the time goes:
time: 564 us; the launch traced here: 561 us
  waiting for transfers between devices  257 us (46%)
  starting transfers between devices  121 us (21%)
  between operations  77.1 us (14%)
  local copies, waits for them, and re-layouts  40.5 us (7%)
  other arithmetic  28.8 us (5%)
  blocking collectives  23.9 us (4%)
  matrix products  13 us (2%)
    all_gather x1, waiting for transfers between devices, side_by_side(): whole = lax.all_gather(both, axis, axis=dim, tiled=True)  87.1 us
    all_to_all x5, waiting for transfers between devices, from_everyone(): return lax.all_to_all(copies, axis, split_axis=0, concat_axis=0, tiled=True)  80.1 us
    ppermute x13, waiting for transfers between devices, swapped(): lax.ppermute(x, axis, [(i, i ^ 1 << bit) for i in range(lax.axis_size(axi...  72.4 us
    all_to_all x5, starting transfers between devices, from_everyone(): return lax.all_to_all(copies, axis, split_axis=0, concat_axis=0, tiled=True)  57.9 us
    ppermute x13, starting transfers between devices, swapped(): lax.ppermute(x, axis, [(i, i ^ 1 << bit) for i in range(lax.axis_size(axi...  52.5 us
    all_to_all x1, blocking collectives, from_everyone(): return lax.all_to_all(copies, axis, split_axis=0, concat_axis=0, tiled=True)  18.9 us
    all_to_all x1, waiting for transfers between devices, turned_blocks(): whole = lax.all_to_all(whole, axes[k], k, k, tiled=True)  17.7 us
  transfers between devices with their start and end apart: 20, of which 15 were waited for; matrix products, arithmetic and copies ran while one was open for 7% of the time, Pallas kernels for 0%

commit v1 on v0

v1 whole, which is shorter than its diff:
```python
import functools

import jax
import jax.numpy as jnp
from jax import lax
from jax.experimental import pallas as pl
from jax.experimental.pallas import tpu as pltpu
from jax.sharding import PartitionSpec as P

STEP = 3
MESH = pl.DeviceIdType.MESH
NE, NY, NZ = 8, 4, 16
NR = NY * NZ
CAP = 256
HELD = 48
D = 2048
F = 384
SHARD = 512
Q = D // NY
ROWS = D // NR
LIST = NE * HELD

beta_first = 0.9
beta_second = 0.999
learning_rate = 0.02
decay_rate = 0.1
adam_epsilon = 1e-08
adasum_epsilon = 1e-12

f32 = jnp.float32
bf16 = jnp.bfloat16
i32 = jnp.int32

X_OFFSETS = (4, 3, 5, 2, 6, 7, 1)
Y_OFFSETS = (2, 1, 3)
Z_OFFSETS = (8, 7, 9, 6, 10, 5, 11, 4, 12, 3, 13, 2, 14, 1, 15)


def iota(shape, dim):
    return lax.broadcasted_iota(i32, shape, dim)


def adam_update(gradient, weight, moment_one, moment_two):
    moment_one = beta_first * moment_one + (1.0 - beta_first) * gradient
    moment_two = beta_second * moment_two + (1.0 - beta_second) * gradient * gradient
    first_hat = moment_one / (1.0 - beta_first**STEP)
    second_hat = moment_two / (1.0 - beta_second**STEP)
    weight = weight - learning_rate * (
        first_hat / (jnp.sqrt(second_hat) + adam_epsilon) + decay_rate * weight
    )
    return (weight, moment_one, moment_two)


def pair_weights(inner, first_square, second_square):
    first = 1.0 - inner / (2.0 * first_square + adasum_epsilon)
    second = 1.0 - inner / (2.0 * second_square + adasum_epsilon)
    return first, second


def four_coefficients(rows):
    g = lambda a, b: rows[4 * a + b : 4 * a + b + 1, :]
    w0, w2 = pair_weights(g(0, 2), g(0, 0), g(2, 2))
    w1, w3 = pair_weights(g(1, 3), g(1, 1), g(3, 3))
    qa = w0 * w0 * g(0, 0) + 2.0 * w0 * w2 * g(0, 2) + w2 * w2 * g(2, 2)
    qb = w1 * w1 * g(1, 1) + 2.0 * w1 * w3 * g(1, 3) + w3 * w3 * g(3, 3)
    qa = jnp.maximum(qa, 0.0)
    qb = jnp.maximum(qb, 0.0)
    pab = w0 * (w1 * g(0, 1) + w3 * g(0, 3)) + w2 * (w1 * g(2, 1) + w3 * g(2, 3))
    va, vb = pair_weights(pab, qa, qb)
    return (va * w0, vb * w1, va * w2, vb * w3)


def ring_coefficients(gram):
    row = iota((NZ, 128), 0)
    lane = iota((NZ, 128), 1)
    coefficient = jnp.ones((NZ, 1), f32)
    for half in (8, 4, 2, 1):
        zero = jnp.zeros_like(gram)
        p_col = jnp.sum(jnp.where(lane == (row + half) % NZ, gram, zero), axis=1, keepdims=True)
        q_col = jnp.sum(jnp.where(lane == row, gram, zero), axis=1, keepdims=True)
        p_row = jnp.sum(
            jnp.where(row == (lane + half) % NZ, gram, zero), axis=0, keepdims=True
        )
        q_row = jnp.sum(jnp.where(row == lane % NZ, gram, zero), axis=0, keepdims=True)
        w_col = 1.0 - p_col / (2.0 * jnp.maximum(q_col, 0.0) + adasum_epsilon)
        w_row = 1.0 - p_row / (2.0 * jnp.maximum(q_row, 0.0) + adasum_epsilon)
        scaled = w_col * gram * w_row
        folded = scaled + pltpu.roll(scaled, half, 1)
        gram = folded + pltpu.roll(folded, half, 0)
        coefficient = coefficient * w_col
    return coefficient


def lanes(row):
    return jnp.concatenate([row] * (F // 128), axis=1)


def wait_bytes(ref, sem):
    pltpu.make_async_copy(ref, ref, sem).wait()


def step_kernel(
    rows_ref,
    count_ref,
    pool_hbm,
    targets_hbm,
    weights_ref,
    out_ref,
    pool_v,
    targets_v,
    held_v,
    pick_v,
    place_v,
    sent_rows,
    got_rows,
    x_v,
    x_got,
    x_turned,
    gate_w,
    up_w,
    act_v,
    deltas,
    grads,
    gram_y,
    item_out,
    item_in,
    tab_y,
    tab_z,
    load_sem,
    send_sem,
    rows_sem,
    gy_sem,
    gp_sem,
    gm_sem,
    up_sem,
    um_sem,
    uy_sem,
    x_sem,
    delta_sem,
    gram_sem,
    item_sem,
    ty_sem,
    tz_sem,
):
    me = lax.axis_index("expert")
    rep = lax.axis_index("replica")
    y = rep // NZ
    z = rep % NZ

    def at_e(off):
        return ((me + off) % NE, rep)

    def at_y(off):
        return (me, ((y + off) % NY) * NZ + z)

    def at_z(off):
        return (me, y * NZ + (z + off) % NZ)

    def send(src, dst, group, recv, device):
        pltpu.make_async_remote_copy(
            src_ref=src,
            dst_ref=dst,
            send_sem=send_sem.at[group],
            recv_sem=recv,
            device_id=device,
            device_id_type=MESH,
        ).start()

    barrier = pltpu.get_barrier_semaphore()
    peers = [at_e(o) for o in X_OFFSETS] + [at_y(o) for o in Y_OFFSETS] + [at_z(1), at_z(NZ - 1)]
    for device in peers:
        pl.semaphore_signal(barrier, inc=1, device_id=device, device_id_type=MESH)

    loads = [
        pltpu.make_async_copy(
            pool_hbm.at[0, :, pl.ds(q * Q, Q)], pool_v.at[q], load_sem.at[q]
        )
        for q in range(NY)
    ]
    loads.append(pltpu.make_async_copy(targets_hbm.at[0, 0], targets_v, load_sem.at[NY]))
    for load in loads:
        load.start()

    gate_w[rep] = weights_ref[0, 0].astype(bf16)
    up_w[rep] = weights_ref[0, 1].astype(bf16)

    pl.semaphore_wait(barrier, len(peers))

    for k, off in enumerate(Y_OFFSETS):
        send(gate_w.at[rep], gate_w.at[rep], 0, gy_sem.at[off - 1], at_y(off))
    send(up_w.at[rep], up_w.at[rep], 1, up_sem.at[0], at_z(1))
    send(up_w.at[rep], up_w.at[rep], 1, um_sem.at[0], at_z(NZ - 1))
    send(gate_w.at[rep], gate_w.at[rep], 0, gp_sem.at[0, 0], at_z(1))
    send(gate_w.at[rep], gate_w.at[rep], 0, gm_sem.at[0, 0], at_z(NZ - 1))
    for off in Y_OFFSETS:
        send(up_w.at[rep], up_w.at[rep], 1, uy_sem.at[0, off - 1], at_y(off))

    for e in range(NE):
        listed = rows_ref[e]
        held_v[e : e + 1, :] = jnp.where(listed // SHARD == me, 1.0, 0.0)
    before = jnp.where(iota((CAP, CAP), 0) < iota((CAP, CAP), 1), 1.0, 0.0).astype(bf16)
    held = held_v[...]
    rank = jnp.dot(held.astype(bf16), before, preferred_element_type=f32)
    held_v[...] = jnp.where(held > 0.5, rank, -1.0)
    for e in range(NE):
        key = jnp.broadcast_to(held_v[e : e + 1, :], (HELD, CAP))
        local = jnp.broadcast_to((rows_ref[e] - me * SHARD + 1).astype(f32), (HELD, CAP))
        match = key == iota((HELD, CAP), 0).astype(f32)
        index = jnp.sum(jnp.where(match, local, 0.0), axis=1, keepdims=True) - 1.0
        pick_v[pl.ds(e * HELD, HELD), :] = jnp.where(
            index == iota((HELD, SHARD), 1).astype(f32), 1.0, 0.0
        ).astype(bf16)

    def gather(i):
        q = (y + (Y_OFFSETS + (0,))[i]) % NY
        found = jnp.dot(pick_v[...], pool_v[q], preferred_element_type=f32).astype(bf16)
        sent_rows[pl.ds(q * NE, NE)] = found.reshape(NE, HELD, Q)
        for j, off in enumerate(X_OFFSETS):
            send(
                sent_rows.at[q * NE + (me + off) % NE],
                got_rows.at[q * NE + me],
                2,
                rows_sem.at[i, j],
                at_e(off),
            )
        got_rows[q * NE + me] = sent_rows[q * NE + me]

    for load in loads:
        load.wait()
    gather(0)

    for off in Y_OFFSETS:
        row = ((y + NY - off) % NY) * NZ + z
        pltpu.make_async_copy(gate_w.at[row], gate_w.at[row], gy_sem.at[off - 1]).wait()
        send(gate_w.at[row], gate_w.at[row], 0, gp_sem.at[0, off], at_z(1))
        send(gate_w.at[row], gate_w.at[row], 0, gm_sem.at[0, off], at_z(NZ - 1))

    gather(1)
    gather(2)
    gather(3)

    own_row = rows_ref[me].astype(f32)
    square = jnp.broadcast_to(own_row, (CAP, CAP))
    sub = iota((CAP, CAP), 0)
    lan = iota((CAP, CAP), 1)
    own_col = jnp.sum(jnp.where(sub == lan, square, 0.0), axis=1, keepdims=True)
    shard_row = rows_ref[me] // SHARD
    shard_col = own_col.astype(i32) // SHARD
    same = jnp.logical_and(jnp.broadcast_to(shard_row, (CAP, CAP)) == shard_col, lan < sub)
    rank_col = jnp.sum(jnp.where(same, 1.0, 0.0), axis=1, keepdims=True)
    place = shard_col * HELD + rank_col.astype(i32)
    place_v[...] = jnp.where(place == iota((CAP, LIST), 1), 1.0, 0.0).astype(bf16)

    def gate_wait(sem, k, off, back):
        row = ((y + NY - off) % NY) * NZ + (z + NZ - k * back) % NZ
        pltpu.make_async_copy(gate_w.at[row], gate_w.at[row], sem.at[k - 1, off]).wait()
        return row

    def up_wait(sem, k, back):
        row = y * NZ + (z + NZ - k * back) % NZ
        pltpu.make_async_copy(up_w.at[row], up_w.at[row], sem.at[k - 1]).wait()
        return row

    def up_across(row, slot):
        for off in Y_OFFSETS:
            send(up_w.at[row], up_w.at[row], 1, uy_sem.at[slot, off - 1], at_y(off))

    def ring(k, plus, minus):
        row = up_wait(up_sem, k, 1)
        if plus:
            send(up_w.at[row], up_w.at[row], 1, up_sem.at[k], at_z(1))
        up_across(row, k)
        if minus is not None:
            row = up_wait(um_sem, k, NZ - 1)
            if minus:
                send(up_w.at[row], up_w.at[row], 1, um_sem.at[k], at_z(NZ - 1))
            up_across(row, k + 8)
        for off in (0,) + Y_OFFSETS:
            row = gate_wait(gp_sem, k, off, 1)
            if plus:
                send(gate_w.at[row], gate_w.at[row], 0, gp_sem.at[k, off], at_z(1))
            if minus is not None:
                row = gate_wait(gm_sem, k, off, NZ - 1)
                if minus:
                    send(gate_w.at[row], gate_w.at[row], 0, gm_sem.at[k, off], at_z(NZ - 1))

    @pl.loop(1, 7)
    def _(k):
        ring(k, True, True)

    ring(7, True, False)
    ring(8, False, None)

    for i, y_off in enumerate(Y_OFFSETS + (0,)):
        q = (y + y_off) % NY
        for j, off in enumerate(X_OFFSETS):
            slot = q * NE + (me + NE - off) % NE
            pltpu.make_async_copy(
                got_rows.at[slot], got_rows.at[slot], rows_sem.at[i, j]
            ).wait()
        block = got_rows[pl.ds(q * NE, NE)].reshape(LIST, Q)
        ordered = jnp.dot(place_v[...], block, preferred_element_type=f32).astype(bf16)
        x_v[q] = ordered
        if y_off:
            send(x_v.at[q], x_got.at[y], 3, x_sem.at[y_off - 1], at_y(y_off))
        else:
            x_got[y] = ordered

    @pl.loop(0, NZ)
    def _(slot):
        back = jnp.where(slot < 9, NZ - slot, slot - 8)
        for off in Y_OFFSETS:
            row = ((y + NY - off) % NY) * NZ + (z + back) % NZ
            pltpu.make_async_copy(up_w.at[row], up_w.at[row], uy_sem.at[slot, off - 1]).wait()

    for m, w in enumerate((gate_w, up_w)):
        total = None
        for q in range(NY):
            part = jnp.dot(
                x_v[q], w[pl.ds(q * NZ, NZ)].reshape(Q, F), preferred_element_type=f32
            )
            total = part if total is None else total + part
        act_v[m] = total

    count = count_ref[...]

    @pl.loop(0, CAP // 32)
    def _(i):
        span = pl.ds(pl.multiple_of(i * 32, 32), 32)
        gate_value = act_v[0, span, :]
        up_value = act_v[1, span, :]
        sigmoid = 1.0 / (1.0 + jnp.exp(-gate_value))
        activated = gate_value * sigmoid
        slope = sigmoid * (1.0 + gate_value * (1.0 - sigmoid))
        live = jnp.where(iota((32, F), 0) + i * 32 < count, 1.0, 0.0)
        residual = (
            (activated * up_value - targets_v[span, :].astype(f32)) * live / count.astype(f32)
        )
        deltas[y, span, :] = (residual * up_value * slope).astype(bf16)
        deltas[NY + y, span, :] = (residual * activated).astype(bf16)

    for m in range(2):
        for off in Y_OFFSETS:
            send(
                deltas.at[m * NY + y],
                deltas.at[m * NY + y],
                4,
                delta_sem.at[m, off - 1],
                at_y(off),
            )

    for off in Y_OFFSETS:
        src = (y + NY - off) % NY
        pltpu.make_async_copy(x_got.at[src], x_got.at[src], x_sem.at[off - 1]).wait()
    for s in range(NY):
        x_turned[s] = x_got[s].T

    for m in range(2):
        for off in Y_OFFSETS:
            src = m * NY + (y + NY - off) % NY
            pltpu.make_async_copy(
                deltas.at[src], deltas.at[src], delta_sem.at[m, off - 1]
            ).wait()
        for s in range(NY):
            grads[m * NY + s] = jnp.dot(
                x_turned[s], deltas[m * NY + s], preferred_element_type=f32
            )
        pairs = [(a, b) for a in range(NY) for b in range(a, NY)]

        def add_products(i, sums):
            span = pl.ds(pl.multiple_of(i * 8, 8), 8)
            parts = [grads[m * NY + s, span, :] for s in range(NY)]
            out = []
            for (a, b), old in zip(pairs, sums):
                product = parts[a] * parts[b]
                for c in range(F // 128):
                    old = old + product[:, c * 128 : c * 128 + 128]
                out.append(old)
            return tuple(out)

        sums = lax.fori_loop(
            0, Q // 8, add_products, tuple(jnp.zeros((8, 128), f32) for _ in pairs)
        )
        for (a, b), value in zip(pairs, sums):
            line = jnp.sum(value, axis=0, keepdims=True)
            gram_y[m * NY + y, 4 * a + b : 4 * a + b + 1, :] = line
            if a != b:
                gram_y[m * NY + y, 4 * b + a : 4 * b + a + 1, :] = line
        for off in Y_OFFSETS:
            send(
                gram_y.at[m * NY + y],
                gram_y.at[m * NY + y],
                5,
                gram_sem.at[m, off - 1],
                at_y(off),
            )

    for m in range(2):
        for off in Y_OFFSETS:
            src = m * NY + (y + NY - off) % NY
            pltpu.make_async_copy(
                gram_y.at[src], gram_y.at[src], gram_sem.at[m, off - 1]
            ).wait()
        table = gram_y[m * NY]
        for s in range(1, NY):
            table = table + gram_y[m * NY + s]
        table = jnp.broadcast_to(jnp.sum(table, axis=1, keepdims=True), (16, 128))
        scale = [lanes(c) for c in four_coefficients(table)]
        for off in Z_OFFSETS + (0,):
            to = (z + off) % NZ
            span = pl.ds(pl.multiple_of(to * ROWS, ROWS), ROWS)
            item = scale[0] * grads[m * NY, span, :]
            for s in range(1, NY):
                item = item + scale[s] * grads[m * NY + s, span, :]
            if off:
                item_out[m * NZ + to] = item.astype(bf16)
                send(
                    item_out.at[m * NZ + to],
                    item_in.at[m * NZ + z],
                    6,
                    item_sem.at[m, off - 1],
                    at_z(off),
                )
            else:
                item_in[m * NZ + z] = item.astype(bf16)

    block = NZ * ROWS
    grams = []
    for m in range(2):
        for off in Z_OFFSETS:
            src = m * NZ + (z + NZ - off) % NZ
            pltpu.make_async_copy(
                item_in.at[src], item_in.at[src], item_sem.at[m, off - 1]
            ).wait()
        items = item_in[pl.ds(m * NZ, NZ)].reshape(block, F)
        product = lax.dot_general(
            items, items, (((1,), (1,)), ((), ())), preferred_element_type=f32
        )
        product = jnp.where(
            iota((block, block), 0) % ROWS == iota((block, block), 1) % ROWS, product, 0.0
        )
        product = jnp.sum(product.reshape(NZ, ROWS, block), axis=1)
        fold = jnp.where(
            iota((block, 128), 0) // ROWS == iota((block, 128), 1) % NZ, 1.0, 0.0
        )
        grams.append(
            jnp.dot(
                product, fold, precision=lax.Precision.HIGHEST, preferred_element_type=f32
            )
        )
    part = iota((8, 128), 1) // 32
    packed = jnp.where(part == 0, grams[0][0:8], 0.0)
    packed = jnp.where(part == 1, grams[0][8:16], packed)
    packed = jnp.where(part == 2, grams[1][0:8], packed)
    packed = jnp.where(part == 3, grams[1][8:16], packed)
    tab_y[y] = packed
    for off in Y_OFFSETS:
        send(tab_y.at[y], tab_y.at[y], 7, ty_sem.at[off - 1], at_y(off))
    for off in Y_OFFSETS:
        src = (y + NY - off) % NY
        pltpu.make_async_copy(tab_y.at[src], tab_y.at[src], ty_sem.at[off - 1]).wait()
    packed = tab_y[0]
    for s in range(1, NY):
        packed = packed + tab_y[s]
    tab_z[z] = packed
    for off in Z_OFFSETS:
        send(tab_z.at[z], tab_z.at[z], 8, tz_sem.at[off - 1], at_z(off))
    for off in Z_OFFSETS:
        src = (z + NZ - off) % NZ
        pltpu.make_async_copy(tab_z.at[src], tab_z.at[src], tz_sem.at[off - 1]).wait()
    packed = tab_z[0]
    for s in range(1, NZ):
        packed = packed + tab_z[s]

    def spread(which):
        one = jnp.where(part == which, packed, 0.0)
        one = one + pltpu.roll(one, 32, 1)
        return one + pltpu.roll(one, 64, 1)

    for m in range(2):
        gram = jnp.concatenate([spread(2 * m), spread(2 * m + 1)], axis=0)
        scale = jnp.broadcast_to(ring_coefficients(gram), (NZ, 128))
        total = None
        for s in range(NZ):
            term = lanes(scale[s : s + 1, :]) * item_in[m * NZ + s].astype(f32)
            total = term if total is None else total + term
        out_ref[m] = total

    wait_bytes(gate_w.at[pl.ds(0, 63)], send_sem.at[0])
    wait_bytes(up_w.at[pl.ds(0, 63)], send_sem.at[1])
    wait_bytes(sent_rows.at[pl.ds(0, 28)], send_sem.at[2])
    wait_bytes(x_v.at[pl.ds(0, 3)], send_sem.at[3])
    wait_bytes(deltas.at[pl.ds(0, 6)], send_sem.at[4])
    wait_bytes(gram_y.at[pl.ds(0, 6)], send_sem.at[5])
    wait_bytes(item_out.at[pl.ds(0, 30)], send_sem.at[6])
    wait_bytes(tab_y.at[pl.ds(0, 3)], send_sem.at[7])
    wait_bytes(tab_z.at[pl.ds(0, 15)], send_sem.at[8])


def combined_gradient(pool, row_index, counts, targets, weights):
    vmem = pl.BlockSpec(memory_space=pltpu.VMEM)
    anywhere = pl.BlockSpec(memory_space=pl.ANY)
    dma = pltpu.SemaphoreType.DMA
    return pl.pallas_call(
        step_kernel,
        out_shape=jax.ShapeDtypeStruct((2, ROWS, F), f32),
        in_specs=[vmem, vmem, anywhere, anywhere, vmem],
        out_specs=vmem,
        scratch_shapes=[
            pltpu.VMEM((NY, SHARD, Q), bf16),
            pltpu.VMEM((CAP, F), bf16),
            pltpu.VMEM((NE, CAP), f32),
            pltpu.VMEM((LIST, SHARD), bf16),
            pltpu.VMEM((CAP, LIST), bf16),
            pltpu.VMEM((NY * NE, HELD, Q), bf16),
            pltpu.VMEM((NY * NE, HELD, Q), bf16),
            pltpu.VMEM((NY, CAP, Q), bf16),
            pltpu.VMEM((NY, CAP, Q), bf16),
            pltpu.VMEM((NY, Q, CAP), bf16),
            pltpu.VMEM((NR, ROWS, F), bf16),
            pltpu.VMEM((NR, ROWS, F), bf16),
            pltpu.VMEM((2, CAP, F), f32),
            pltpu.VMEM((2 * NY, CAP, F), bf16),
            pltpu.VMEM((2 * NY, Q, F), f32),
            pltpu.VMEM((2 * NY, 16, 128), f32),
            pltpu.VMEM((2 * NZ, ROWS, F), bf16),
            pltpu.VMEM((2 * NZ, ROWS, F), bf16),
            pltpu.VMEM((NY, 8, 128), f32),
            pltpu.VMEM((NZ, 8, 128), f32),
            dma((NY + 1,)),
            dma((9,)),
            dma((NY, NE - 1)),
            dma((NY - 1,)),
            dma((8, NY)),
            dma((7, NY)),
            dma((8,)),
            dma((7,)),
            dma((NZ, NY - 1)),
            dma((NY - 1,)),
            dma((2, NY - 1)),
            dma((2, NY - 1)),
            dma((2, NZ - 1)),
            dma((NY - 1,)),
            dma((NZ - 1,)),
        ],
        compiler_params=pltpu.CompilerParams(
            collective_id=0, has_side_effects=True, vmem_limit_bytes=56 * 1024 * 1024
        ),
    )(row_index, counts, pool, targets, weights)


def shards(pool, row_index, counts, targets, weights, first_moment, second_moment):
    combined = combined_gradient(pool, row_index, counts, targets, weights)
    new_weight, moment_one, moment_two = adam_update(
        combined, weights[0], first_moment[0], second_moment[0]
    )
    return (new_weight[None], moment_one[None], moment_two[None])


def solution(mesh):
    in_specs = (
        P("replica", "expert", None),
        P(None, "replica", None),
        P("expert", "replica"),
        P("expert", "replica", None, None),
        P("expert", None, "replica", None),
        P("expert", None, "replica", None),
        P("expert", None, "replica", None),
    )
    out_specs = (P("expert", None, "replica", None),) * 3
    return jax.shard_map(
        shards, mesh=mesh, in_specs=in_specs, out_specs=out_specs, check_vma=False
    )
```

time: 564 us -> 125 us (0.22)
  the two profiles are of different devices: /device:TPU:4 before, /device:TPU:8 now
where the time goes in v1:
time: 125 us
  Pallas kernels  122 us (98%)
  other arithmetic  1.67 us (1%)
  between operations  1.38 us (1%)
    pallas_call x1, Pallas kernels, combined_gradient(): pl.pallas_call(step_kernel, out_shape=jax.ShapeDtypeStruct((2, ROWS, F),...  122 us

profile of v1, /device:TPU:8, one launch (start us, length us, event | category | flops | bytes accessed | tf_op | source)
XLA Modules:
  0.0 124.8 jit_solution(13902303945974552688)
XLA Ops:
  0.6 0.0 copy-start
  0.6 0.0 copy-start.1
  0.7 0.0 copy-start.2
  1.4 121.8 %shard_map.94 = f32[2,32,384]{2,1,0:T(8,128)} custom-call(s32[8,1,256]{2,1,0:T(1,128)} %rows_ref.1, s32[1,1]{1,0:T(1,128)S(6)} %copy.10.count_ref, bf16[1,512,2048]{2,1,0:T(8,128)(2,1)} %pool_hbm.1, bf16[1,1,256,384]{3,2,1,0:T(8,128)(2,1)} %targets_hbm.1, f32[1,2,32,384]{3,2,1,0:T(8,128)} %weights_ref.1), custom_call_target="tpu_custom_call" | custom-call | tf_op jit(solution)/shard_map/pallas_call | solution.py:504
  123.1 0.0 copy-done
  123.1 0.0 copy-done.1
  123.1 0.0 copy-done.2
  123.1 1.7 %fusion.5 = (f32[1,2,32,384]{3,2,1,0:T(8,128)}, f32[1,2,32,384]{3,2,1,0:T(8,128)}, f32[1,2,32,384]{3,2,1,0:T(8,128)}) fusion(f32[2,32,384]{2,1,0:T(8,128)} %shard_map.94, f32[1,2,32,384]{3,2,1,0:T(8,128)S(1)} %copy-done.1, f32[1,2,32,384]{3,2,1,0:T(8,128)S(1)} %copy-done.2, f32[1,2,32,384]{3,2,1,0:T(8,128)S(1)} %copy-done), kind=kLoop, calls=%fused_computation.9 | loop fusion | flops 368640 | bytes 688128 | tf_op jit(solution)/shard_map/broadcast_in_dim | solution.py:557
Async XLA Ops:
  0.6 122.5 %copy-start = (f32[1,2,32,384]{3,2,1,0:T(8,128)S(1)}, f32[1,2,32,384]{3,2,1,0:T(8,128)}, u32[]{:S(2)}) copy-start(f32[1,2,32,384]{3,2,1,0:T(8,128)} %weights_ref.1) | copy-start | bytes 294916
  0.6 122.5 %copy-start.1 = (f32[1,2,32,384]{3,2,1,0:T(8,128)S(1)}, f32[1,2,32,384]{3,2,1,0:T(8,128)}, u32[]{:S(2)}) copy-start(f32[1,2,32,384]{3,2,1,0:T(8,128)} %param.13) | copy-start | bytes 294916
  0.7 122.5 %copy-start.2 = (f32[1,2,32,384]{3,2,1,0:T(8,128)S(1)}, f32[1,2,32,384]{3,2,1,0:T(8,128)}, u32[]{:S(2)}) copy-start(f32[1,2,32,384]{3,2,1,0:T(8,128)} %param.12) | copy-start | bytes 294916

commit v2 on v1

--- a/solution.py
+++ b/solution.py
@@ -19,6 +19,9 @@
 Q = D // NY
 ROWS = D // NR
 LIST = NE * HELD
+HALF = CAP // 2
+BOTH = 2 * F
+FIRST = 512
 
 beta_first = 0.9
 beta_second = 0.999
@@ -93,10 +96,6 @@
 
 def lanes(row):
     return jnp.concatenate([row] * (F // 128), axis=1)
-
-
-def wait_bytes(ref, sem):
-    pltpu.make_async_copy(ref, ref, sem).wait()
 
 
 def step_kernel(
@@ -166,6 +165,9 @@
             device_id_type=MESH,
         ).start()
 
+    def arrive(ref, sem, group):
+        pltpu.make_async_copy(ref, ref, sem).wait()
+
     barrier = pltpu.get_barrier_semaphore()
     peers = [at_e(o) for o in X_OFFSETS] + [at_y(o) for o in Y_OFFSETS] + [at_z(1), at_z(NZ - 1)]
     for device in peers:
@@ -181,19 +183,9 @@
     for load in loads:
         load.start()
 
-    gate_w[rep] = weights_ref[0, 0].astype(bf16)
-    up_w[rep] = weights_ref[0, 1].astype(bf16)
-
-    pl.semaphore_wait(barrier, len(peers))
-
-    for k, off in enumerate(Y_OFFSETS):
-        send(gate_w.at[rep], gate_w.at[rep], 0, gy_sem.at[off - 1], at_y(off))
-    send(up_w.at[rep], up_w.at[rep], 1, up_sem.at[0], at_z(1))
-    send(up_w.at[rep], up_w.at[rep], 1, um_sem.at[0], at_z(NZ - 1))
-    send(gate_w.at[rep], gate_w.at[rep], 0, gp_sem.at[0, 0], at_z(1))
-    send(gate_w.at[rep], gate_w.at[rep], 0, gm_sem.at[0, 0], at_z(NZ - 1))
-    for off in Y_OFFSETS:
-        send(up_w.at[rep], up_w.at[rep], 1, uy_sem.at[0, off - 1], at_y(off))
+    gate_w[rep, :, pl.ds(0, F)] = weights_ref[0, 0].astype(bf16)
+    gate_w[rep, :, pl.ds(F, FIRST - F)] = weights_ref[0, 1, :, pl.ds(0, FIRST - F)].astype(bf16)
+    up_w[rep] = weights_ref[0, 1, :, pl.ds(FIRST - F, BOTH - FIRST)].astype(bf16)
 
     for e in range(NE):
         listed = rows_ref[e]
@@ -211,6 +203,17 @@
             index == iota((HELD, SHARD), 1).astype(f32), 1.0, 0.0
         ).astype(bf16)
 
+    pl.semaphore_wait(barrier, len(peers))
+
+    for off in Y_OFFSETS:
+        send(gate_w.at[rep], gate_w.at[rep], 0, gy_sem.at[off - 1], at_y(off))
+    send(up_w.at[rep], up_w.at[rep], 1, up_sem.at[0], at_z(1))
+    send(up_w.at[rep], up_w.at[rep], 1, um_sem.at[0], at_z(NZ - 1))
+    send(gate_w.at[rep], gate_w.at[rep], 0, gp_sem.at[0, 0], at_z(1))
+    send(gate_w.at[rep], gate_w.at[rep], 0, gm_sem.at[0, 0], at_z(NZ - 1))
+    for off in Y_OFFSETS:
+        send(up_w.at[rep], up_w.at[rep], 1, uy_sem.at[0, off - 1], at_y(off))
+
     def gather(i):
         q = (y + (Y_OFFSETS + (0,))[i]) % NY
         found = jnp.dot(pick_v[...], pool_v[q], preferred_element_type=f32).astype(bf16)
@@ -225,52 +228,56 @@
             )
         got_rows[q * NE + me] = sent_rows[q * NE + me]
 
-    for load in loads:
-        load.wait()
-    gather(0)
-
-    for off in Y_OFFSETS:
-        row = ((y + NY - off) % NY) * NZ + z
-        pltpu.make_async_copy(gate_w.at[row], gate_w.at[row], gy_sem.at[off - 1]).wait()
-        send(gate_w.at[row], gate_w.at[row], 0, gp_sem.at[0, off], at_z(1))
-        send(gate_w.at[row], gate_w.at[row], 0, gm_sem.at[0, off], at_z(NZ - 1))
-
-    gather(1)
-    gather(2)
-    gather(3)
-
-    own_row = rows_ref[me].astype(f32)
-    square = jnp.broadcast_to(own_row, (CAP, CAP))
-    sub = iota((CAP, CAP), 0)
-    lan = iota((CAP, CAP), 1)
-    own_col = jnp.sum(jnp.where(sub == lan, square, 0.0), axis=1, keepdims=True)
-    shard_row = rows_ref[me] // SHARD
-    shard_col = own_col.astype(i32) // SHARD
-    same = jnp.logical_and(jnp.broadcast_to(shard_row, (CAP, CAP)) == shard_col, lan < sub)
-    rank_col = jnp.sum(jnp.where(same, 1.0, 0.0), axis=1, keepdims=True)
-    place = shard_col * HELD + rank_col.astype(i32)
-    place_v[...] = jnp.where(place == iota((CAP, LIST), 1), 1.0, 0.0).astype(bf16)
+    def own_places():
+        own_row = rows_ref[me].astype(f32)
+        square = jnp.broadcast_to(own_row, (CAP, CAP))
+        sub = iota((CAP, CAP), 0)
+        lan = iota((CAP, CAP), 1)
+        own_col = jnp.sum(jnp.where(sub == lan, square, 0.0), axis=1, keepdims=True)
+        shard_row = rows_ref[me] // SHARD
+        shard_col = own_col.astype(i32) // SHARD
+        same = jnp.logical_and(
+            jnp.broadcast_to(shard_row, (CAP, CAP)) == shard_col, lan < sub
+        )
+        rank_col = jnp.sum(jnp.where(same, 1.0, 0.0), axis=1, keepdims=True)
+        place = shard_col * HELD + rank_col.astype(i32)
+        place_v[...] = jnp.where(place == iota((CAP, LIST), 1), 1.0, 0.0).astype(bf16)
+
+    def order_rows(i):
+        y_off = (Y_OFFSETS + (0,))[i]
+        q = (y + y_off) % NY
+        for j, off in enumerate(X_OFFSETS):
+            slot = q * NE + (me + NE - off) % NE
+            arrive(got_rows.at[slot], rows_sem.at[i, j], 2)
+        block = got_rows[pl.ds(q * NE, NE)].reshape(LIST, Q)
+        ordered = jnp.dot(place_v[...], block, preferred_element_type=f32).astype(bf16)
+        x_v[q] = ordered
+        if y_off:
+            send(x_v.at[q], x_got.at[y], 3, x_sem.at[y_off - 1], at_y(y_off))
+        else:
+            x_got[y] = ordered
 
     def gate_wait(sem, k, off, back):
         row = ((y + NY - off) % NY) * NZ + (z + NZ - k * back) % NZ
-        pltpu.make_async_copy(gate_w.at[row], gate_w.at[row], sem.at[k - 1, off]).wait()
+        arrive(gate_w.at[row], sem.at[k - 1, off], 0)
         return row
 
     def up_wait(sem, k, back):
         row = y * NZ + (z + NZ - k * back) % NZ
-        pltpu.make_async_copy(up_w.at[row], up_w.at[row], sem.at[k - 1]).wait()
+        arrive(up_w.at[row], sem.at[k - 1], 1)
         return row
 
     def up_across(row, slot):
         for off in Y_OFFSETS:
             send(up_w.at[row], up_w.at[row], 1, uy_sem.at[slot, off - 1], at_y(off))
 
-    def ring(k, plus, minus):
+    def ring(k):
+        plus, minus = k < 8, k < 7
         row = up_wait(up_sem, k, 1)
         if plus:
             send(up_w.at[row], up_w.at[row], 1, up_sem.at[k], at_z(1))
         up_across(row, k)
-        if minus is not None:
+        if plus:
             row = up_wait(um_sem, k, NZ - 1)
             if minus:
                 send(up_w.at[row], up_w.at[row], 1, um_sem.at[k], at_z(NZ - 1))
@@ -279,93 +286,104 @@
             row = gate_wait(gp_sem, k, off, 1)
             if plus:
                 send(gate_w.at[row], gate_w.at[row], 0, gp_sem.at[k, off], at_z(1))
-            if minus is not None:
                 row = gate_wait(gm_sem, k, off, NZ - 1)
-                if minus:
-                    send(gate_w.at[row], gate_w.at[row], 0, gm_sem.at[k, off], at_z(NZ - 1))
-
-    @pl.loop(1, 7)
-    def _(k):
-        ring(k, True, True)
-
-    ring(7, True, False)
-    ring(8, False, None)
-
-    for i, y_off in enumerate(Y_OFFSETS + (0,)):
-        q = (y + y_off) % NY
-        for j, off in enumerate(X_OFFSETS):
-            slot = q * NE + (me + NE - off) % NE
-            pltpu.make_async_copy(
-                got_rows.at[slot], got_rows.at[slot], rows_sem.at[i, j]
-            ).wait()
-        block = got_rows[pl.ds(q * NE, NE)].reshape(LIST, Q)
-        ordered = jnp.dot(place_v[...], block, preferred_element_type=f32).astype(bf16)
-        x_v[q] = ordered
-        if y_off:
-            send(x_v.at[q], x_got.at[y], 3, x_sem.at[y_off - 1], at_y(y_off))
-        else:
-            x_got[y] = ordered
+            if minus:
+                send(gate_w.at[row], gate_w.at[row], 0, gm_sem.at[k, off], at_z(NZ - 1))
+
+    for load in loads:
+        load.wait()
+    gather(0)
+    for off in Y_OFFSETS:
+        row = ((y + NY - off) % NY) * NZ + z
+        arrive(gate_w.at[row], gy_sem.at[off - 1], 0)
+        send(gate_w.at[row], gate_w.at[row], 0, gp_sem.at[0, off], at_z(1))
+        send(gate_w.at[row], gate_w.at[row], 0, gm_sem.at[0, off], at_z(NZ - 1))
+    gather(1)
+    ring(1)
+    gather(2)
+    gather(3)
+    own_places()
+    ring(2)
+    order_rows(0)
+    ring(3)
+    ring(4)
+    order_rows(1)
+    ring(5)
+    order_rows(2)
+    ring(6)
+    ring(7)
+    ring(8)
+    order_rows(3)
 
     @pl.loop(0, NZ)
     def _(slot):
         back = jnp.where(slot < 9, NZ - slot, slot - 8)
         for off in Y_OFFSETS:
             row = ((y + NY - off) % NY) * NZ + (z + back) % NZ
-            pltpu.make_async_copy(up_w.at[row], up_w.at[row], uy_sem.at[slot, off - 1]).wait()
-
-    for m, w in enumerate((gate_w, up_w)):
-        total = None
-        for q in range(NY):
-            part = jnp.dot(
-                x_v[q], w[pl.ds(q * NZ, NZ)].reshape(Q, F), preferred_element_type=f32
-            )
-            total = part if total is None else total + part
-        act_v[m] = total
+            arrive(up_w.at[row], uy_sem.at[slot, off - 1], 1)
 
     count = count_ref[...]
 
-    @pl.loop(0, CAP // 32)
-    def _(i):
-        span = pl.ds(pl.multiple_of(i * 32, 32), 32)
-        gate_value = act_v[0, span, :]
-        up_value = act_v[1, span, :]
-        sigmoid = 1.0 / (1.0 + jnp.exp(-gate_value))
-        activated = gate_value * sigmoid
-        slope = sigmoid * (1.0 + gate_value * (1.0 - sigmoid))
-        live = jnp.where(iota((32, F), 0) + i * 32 < count, 1.0, 0.0)
-        residual = (
-            (activated * up_value - targets_v[span, :].astype(f32)) * live / count.astype(f32)
-        )
-        deltas[y, span, :] = (residual * up_value * slope).astype(bf16)
-        deltas[NY + y, span, :] = (residual * activated).astype(bf16)
-
-    for m in range(2):
+    def send_delta(m, half):
+        span = pl.ds(half * HALF, HALF)
         for off in Y_OFFSETS:
             send(
-                deltas.at[m * NY + y],
-                deltas.at[m * NY + y],
+                deltas.at[m * NY + y, span],
+                deltas.at[m * NY + y, span],
                 4,
-                delta_sem.at[m, off - 1],
+                delta_sem.at[2 * m + half, off - 1],
                 at_y(off),
             )
 
+    for half in range(2):
+        for w, columns in ((gate_w, pl.ds(0, FIRST)), (up_w, pl.ds(FIRST, BOTH - FIRST))):
+            total = None
+            for q in range(NY):
+                part = jnp.dot(
+                    x_v[q, pl.ds(half * HALF, HALF)],
+                    w[pl.ds(q * NZ, NZ)].reshape(Q, w.shape[2]),
+                    preferred_element_type=f32,
+                )
+                total = part if total is None else total + part
+            act_v[:, columns] = total
+
+        @pl.loop(0, HALF // 32)
+        def _(i):
+            from_act = pl.ds(pl.multiple_of(i * 32, 32), 32)
+            span = pl.ds(pl.multiple_of(half * HALF + i * 32, 32), 32)
+            gate_value = act_v[from_act, 0:F]
+            up_value = act_v[from_act, F:BOTH]
+            sigmoid = 1.0 / (1.0 + jnp.exp(-gate_value))
+            activated = gate_value * sigmoid
+            slope = sigmoid * (1.0 + gate_value * (1.0 - sigmoid))
+            live = jnp.where(iota((32, F), 0) + (half * HALF + i * 32) < count, 1.0, 0.0)
+            residual = (
+                (activated * up_value - targets_v[span, :].astype(f32))
+                * live
+                / count.astype(f32)
+            )
+            deltas[y, span, :] = (residual * up_value * slope).astype(bf16)
+            deltas[NY + y, span, :] = (residual * activated).astype(bf16)
+
+        send_delta(0, half)
+
     for off in Y_OFFSETS:
         src = (y + NY - off) % NY
-        pltpu.make_async_copy(x_got.at[src], x_got.at[src], x_sem.at[off - 1]).wait()
+        arrive(x_got.at[src], x_sem.at[off - 1], 3)
     for s in range(NY):
         x_turned[s] = x_got[s].T
 
+    pairs = [(a, b) for a in range(NY) for b in range(a, NY)]
     for m in range(2):
         for off in Y_OFFSETS:
             src = m * NY + (y + NY - off) % NY
-            pltpu.make_async_copy(
-                deltas.at[src], deltas.at[src], delta_sem.at[m, off - 1]
-            ).wait()
+            for half in range(2):
+                span = pl.ds(half * HALF, HALF)
+                arrive(deltas.at[src, span], delta_sem.at[2 * m + half, off - 1], 4)
         for s in range(NY):
             grads[m * NY + s] = jnp.dot(
                 x_turned[s], deltas[m * NY + s], preferred_element_type=f32
             )
-        pairs = [(a, b) for a in range(NY) for b in range(a, NY)]
 
         def add_products(i, sums):
             span = pl.ds(pl.multiple_of(i * 8, 8), 8)
@@ -394,13 +412,13 @@
                 gram_sem.at[m, off - 1],
                 at_y(off),
             )
-
-    for m in range(2):
+        if m == 0:
+            send_delta(1, 0)
+            send_delta(1, 1)
+
         for off in Y_OFFSETS:
             src = m * NY + (y + NY - off) % NY
-            pltpu.make_async_copy(
-                gram_y.at[src], gram_y.at[src], gram_sem.at[m, off - 1]
-            ).wait()
+            arrive(gram_y.at[src], gram_sem.at[m, off - 1], 5)
         table = gram_y[m * NY]
         for s in range(1, NY):
             table = table + gram_y[m * NY + s]
@@ -425,13 +443,12 @@
                 item_in[m * NZ + z] = item.astype(bf16)
 
     block = NZ * ROWS
-    grams = []
+    wide_row = iota((NZ, 128), 0)
+    wide_lane = iota((NZ, 128), 1)
     for m in range(2):
         for off in Z_OFFSETS:
             src = m * NZ + (z + NZ - off) % NZ
-            pltpu.make_async_copy(
-                item_in.at[src], item_in.at[src], item_sem.at[m, off - 1]
-            ).wait()
+            arrive(item_in.at[src], item_sem.at[m, off - 1], 6)
         items = item_in[pl.ds(m * NZ, NZ)].reshape(block, F)
         product = lax.dot_general(
             items, items, (((1,), (1,)), ((), ())), preferred_element_type=f32
@@ -443,42 +460,34 @@
         fold = jnp.where(
             iota((block, 128), 0) // ROWS == iota((block, 128), 1) % NZ, 1.0, 0.0
         )
-        grams.append(
-            jnp.dot(
-                product, fold, precision=lax.Precision.HIGHEST, preferred_element_type=f32
-            )
-        )
-    part = iota((8, 128), 1) // 32
-    packed = jnp.where(part == 0, grams[0][0:8], 0.0)
-    packed = jnp.where(part == 1, grams[0][8:16], packed)
-    packed = jnp.where(part == 2, grams[1][0:8], packed)
-    packed = jnp.where(part == 3, grams[1][8:16], packed)
-    tab_y[y] = packed
+        gram = jnp.dot(
+            product, fold, precision=lax.Precision.HIGHEST, preferred_element_type=f32
+        )
+        packed = jnp.where(wide_row % 8 == wide_lane // NZ, gram, 0.0)
+        tab_y[y, pl.ds(2 * m, 2), :] = jnp.sum(packed.reshape(2, 8, 128), axis=1)
     for off in Y_OFFSETS:
         send(tab_y.at[y], tab_y.at[y], 7, ty_sem.at[off - 1], at_y(off))
     for off in Y_OFFSETS:
         src = (y + NY - off) % NY
-        pltpu.make_async_copy(tab_y.at[src], tab_y.at[src], ty_sem.at[off - 1]).wait()
-    packed = tab_y[0]
-    for s in range(1, NY):
-        packed = packed + tab_y[s]
-    tab_z[z] = packed
+        arrive(tab_y.at[src], ty_sem.at[off - 1], 7)
+    tab_z[z] = jnp.sum(tab_y[...], axis=0)
     for off in Z_OFFSETS:
         send(tab_z.at[z], tab_z.at[z], 8, tz_sem.at[off - 1], at_z(off))
     for off in Z_OFFSETS:
         src = (z + NZ - off) % NZ
-        pltpu.make_async_copy(tab_z.at[src], tab_z.at[src], tz_sem.at[off - 1]).wait()
-    packed = tab_z[0]
-    for s in range(1, NZ):
-        packed = packed + tab_z[s]
-
-    def spread(which):
-        one = jnp.where(part == which, packed, 0.0)
-        one = one + pltpu.roll(one, 32, 1)
-        return one + pltpu.roll(one, 64, 1)
-
+        arrive(tab_z.at[src], tz_sem.at[off - 1], 8)
+    table = jnp.sum(tab_z[...], axis=0)
     for m in range(2):
-        gram = jnp.concatenate([spread(2 * m), spread(2 * m + 1)], axis=0)
+        gram = jnp.concatenate(
+            [
+                jnp.broadcast_to(table[j : j + 1, :], (8, 128))
+                for j in (2 * m, 2 * m + 1)
+            ],
+            axis=0,
+        )
+        gram = jnp.where(wide_row % 8 == wide_lane // NZ, gram, 0.0)
+        for turn in (16, 32, 64):
+            gram = gram + pltpu.roll(gram, turn, 1)
         scale = jnp.broadcast_to(ring_coefficients(gram), (NZ, 128))
         total = None
         for s in range(NZ):
@@ -486,15 +495,15 @@
             total = term if total is None else total + term
         out_ref[m] = total
 
-    wait_bytes(gate_w.at[pl.ds(0, 63)], send_sem.at[0])
-    wait_bytes(up_w.at[pl.ds(0, 63)], send_sem.at[1])
-    wait_bytes(sent_rows.at[pl.ds(0, 28)], send_sem.at[2])
-    wait_bytes(x_v.at[pl.ds(0, 3)], send_sem.at[3])
-    wait_bytes(deltas.at[pl.ds(0, 6)], send_sem.at[4])
-    wait_bytes(gram_y.at[pl.ds(0, 6)], send_sem.at[5])
-    wait_bytes(item_out.at[pl.ds(0, 30)], send_sem.at[6])
-    wait_bytes(tab_y.at[pl.ds(0, 3)], send_sem.at[7])
-    wait_bytes(tab_z.at[pl.ds(0, 15)], send_sem.at[8])
+    arrive(gate_w.at[pl.ds(0, 63)], send_sem.at[0], 0)
+    arrive(up_w.at[pl.ds(0, 63)], send_sem.at[1], 1)
+    arrive(sent_rows.at[pl.ds(0, 28)], send_sem.at[2], 2)
+    arrive(x_v.at[pl.ds(0, 3)], send_sem.at[3], 3)
+    arrive(deltas.at[pl.ds(0, 6)], send_sem.at[4], 4)
+    arrive(gram_y.at[pl.ds(0, 6)], send_sem.at[5], 5)
+    arrive(item_out.at[pl.ds(0, 30)], send_sem.at[6], 6)
+    arrive(tab_y.at[pl.ds(0, 3)], send_sem.at[7], 7)
+    arrive(tab_z.at[pl.ds(0, 15)], send_sem.at[8], 8)
 
 
 def combined_gradient(pool, row_index, counts, targets, weights):
@@ -517,16 +526,16 @@
             pltpu.VMEM((NY, CAP, Q), bf16),
             pltpu.VMEM((NY, CAP, Q), bf16),
             pltpu.VMEM((NY, Q, CAP), bf16),
-            pltpu.VMEM((NR, ROWS, F), bf16),
-            pltpu.VMEM((NR, ROWS, F), bf16),
-            pltpu.VMEM((2, CAP, F), f32),
+            pltpu.VMEM((NR, ROWS, FIRST), bf16),
+            pltpu.VMEM((NR, ROWS, BOTH - FIRST), bf16),
+            pltpu.VMEM((HALF, BOTH), f32),
             pltpu.VMEM((2 * NY, CAP, F), bf16),
             pltpu.VMEM((2 * NY, Q, F), f32),
             pltpu.VMEM((2 * NY, 16, 128), f32),
             pltpu.VMEM((2 * NZ, ROWS, F), bf16),
             pltpu.VMEM((2 * NZ, ROWS, F), bf16),
-            pltpu.VMEM((NY, 8, 128), f32),
-            pltpu.VMEM((NZ, 8, 128), f32),
+            pltpu.VMEM((NY, 4, 128), f32),
+            pltpu.VMEM((NZ, 4, 128), f32),
             dma((NY + 1,)),
             dma((9,)),
             dma((NY, NE - 1)),
@@ -537,7 +546,7 @@
             dma((7,)),
             dma((NZ, NY - 1)),
             dma((NY - 1,)),
-            dma((2, NY - 1)),
+            dma((4, NY - 1)),
             dma((2, NY - 1)),
             dma((2, NZ - 1)),
             dma((NY - 1,)),

time: 125 us -> 110 us (0.88)
  Pallas kernels: 122 us -> 107 us
    pallas_call x1, Pallas kernels: 122 us -> 107 us  [combined_gradient(): pl.pallas_call(step_kernel, out_shape=jax.ShapeDtypeStruct((2, ROWS, F),...]
where the time goes in v2:
time: 110 us
  Pallas kernels  107 us (97%)
  other arithmetic  1.67 us (2%)
  between operations  1.38 us (1%)
    pallas_call x1, Pallas kernels, combined_gradient(): pl.pallas_call(step_kernel, out_shape=jax.ShapeDtypeStruct((2, ROWS, F),...  107 us

profile of v2, /device:TPU:8, one launch (start us, length us, event | category | flops | bytes accessed | tf_op | source)
XLA Modules:
  0.0 109.7 jit_solution(7291341259593106623)
XLA Ops:
  0.6 0.0 copy-start
  0.6 0.0 copy-start.1
  0.7 0.0 copy-start.2
  1.4 106.7 %shard_map.94 = f32[2,32,384]{2,1,0:T(8,128)} custom-call(s32[8,1,256]{2,1,0:T(1,128)} %rows_ref.1, s32[1,1]{1,0:T(1,128)S(6)} %copy.10.count_ref, bf16[1,512,2048]{2,1,0:T(8,128)(2,1)} %pool_hbm.1, bf16[1,1,256,384]{3,2,1,0:T(8,128)(2,1)} %targets_hbm.1, f32[1,2,32,384]{3,2,1,0:T(8,128)} %weights_ref.1), custom_call_target="tpu_custom_call" | custom-call | tf_op jit(solution)/shard_map/pallas_call | solution.py:513
  108.0 0.0 copy-done
  108.1 0.0 copy-done.1
  108.1 0.0 copy-done.2
  108.1 1.7 %fusion.5 = (f32[1,2,32,384]{3,2,1,0:T(8,128)}, f32[1,2,32,384]{3,2,1,0:T(8,128)}, f32[1,2,32,384]{3,2,1,0:T(8,128)}) fusion(f32[2,32,384]{2,1,0:T(8,128)} %shard_map.94, f32[1,2,32,384]{3,2,1,0:T(8,128)S(1)} %copy-done.1, f32[1,2,32,384]{3,2,1,0:T(8,128)S(1)} %copy-done.2, f32[1,2,32,384]{3,2,1,0:T(8,128)S(1)} %copy-done), kind=kLoop, calls=%fused_computation.9 | loop fusion | flops 368640 | bytes 688128 | tf_op jit(solution)/shard_map/broadcast_in_dim | solution.py:566
Async XLA Ops:
  0.6 107.4 %copy-start = (f32[1,2,32,384]{3,2,1,0:T(8,128)S(1)}, f32[1,2,32,384]{3,2,1,0:T(8,128)}, u32[]{:S(2)}) copy-start(f32[1,2,32,384]{3,2,1,0:T(8,128)} %weights_ref.1) | copy-start | bytes 294916
  0.6 107.4 %copy-start.1 = (f32[1,2,32,384]{3,2,1,0:T(8,128)S(1)}, f32[1,2,32,384]{3,2,1,0:T(8,128)}, u32[]{:S(2)}) copy-start(f32[1,2,32,384]{3,2,1,0:T(8,128)} %param.13) | copy-start | bytes 294916
  0.7 107.4 %copy-start.2 = (f32[1,2,32,384]{3,2,1,0:T(8,128)S(1)}, f32[1,2,32,384]{3,2,1,0:T(8,128)}, u32[]{:S(2)}) copy-start(f32[1,2,32,384]{3,2,1,0:T(8,128)} %param.12) | copy-start | bytes 294916

commit v3 on v2

--- a/solution.py
+++ b/solution.py
@@ -292,28 +292,37 @@
 
     for load in loads:
         load.wait()
-    gather(0)
+    for i in range(NY):
+        gather(i)
+    own_places()
     for off in Y_OFFSETS:
         row = ((y + NY - off) % NY) * NZ + z
         arrive(gate_w.at[row], gy_sem.at[off - 1], 0)
         send(gate_w.at[row], gate_w.at[row], 0, gp_sem.at[0, off], at_z(1))
         send(gate_w.at[row], gate_w.at[row], 0, gm_sem.at[0, off], at_z(NZ - 1))
-    gather(1)
     ring(1)
-    gather(2)
-    gather(3)
-    own_places()
     ring(2)
     order_rows(0)
     ring(3)
+    order_rows(1)
     ring(4)
-    order_rows(1)
     ring(5)
     order_rows(2)
     ring(6)
     ring(7)
     ring(8)
     order_rows(3)
+
+    def multiply(w, columns, slots):
+        total = None
+        for q in range(NY):
+            part = jnp.dot(
+                x_v[q, slots], w[pl.ds(q * NZ, NZ)].reshape(Q, w.shape[2]), preferred_element_type=f32
+            )
+            total = part if total is None else total + part
+        act_v[slots, columns] = total
+
+    multiply(gate_w, pl.ds(0, FIRST), pl.ds(0, CAP))
 
     @pl.loop(0, NZ)
     def _(slot):
@@ -336,23 +345,13 @@
             )
 
     for half in range(2):
-        for w, columns in ((gate_w, pl.ds(0, FIRST)), (up_w, pl.ds(FIRST, BOTH - FIRST))):
-            total = None
-            for q in range(NY):
-                part = jnp.dot(
-                    x_v[q, pl.ds(half * HALF, HALF)],
-                    w[pl.ds(q * NZ, NZ)].reshape(Q, w.shape[2]),
-                    preferred_element_type=f32,
-                )
-                total = part if total is None else total + part
-            act_v[:, columns] = total
+        multiply(up_w, pl.ds(FIRST, BOTH - FIRST), pl.ds(half * HALF, HALF))
 
         @pl.loop(0, HALF // 32)
         def _(i):
-            from_act = pl.ds(pl.multiple_of(i * 32, 32), 32)
             span = pl.ds(pl.multiple_of(half * HALF + i * 32, 32), 32)
-            gate_value = act_v[from_act, 0:F]
-            up_value = act_v[from_act, F:BOTH]
+            gate_value = act_v[span, 0:F]
+            up_value = act_v[span, F:BOTH]
             sigmoid = 1.0 / (1.0 + jnp.exp(-gate_value))
             activated = gate_value * sigmoid
             slope = sigmoid * (1.0 + gate_value * (1.0 - sigmoid))
@@ -528,7 +527,7 @@
             pltpu.VMEM((NY, Q, CAP), bf16),
             pltpu.VMEM((NR, ROWS, FIRST), bf16),
             pltpu.VMEM((NR, ROWS, BOTH - FIRST), bf16),
-            pltpu.VMEM((HALF, BOTH), f32),
+            pltpu.VMEM((CAP, BOTH), f32),
             pltpu.VMEM((2 * NY, CAP, F), bf16),
             pltpu.VMEM((2 * NY, Q, F), f32),
             pltpu.VMEM((2 * NY, 16, 128), f32),

time: 110 us -> 110 us (level)
  the two profiles are of different devices: /device:TPU:8 before, /device:TPU:2 now
where the time goes in v3:
time: 110 us
  Pallas kernels  106 us (96%)
  other arithmetic  1.67 us (2%)
  between operations  1.38 us (1%)
    pallas_call x1, Pallas kernels, combined_gradient(): pl.pallas_call(step_kernel, out_shape=jax.ShapeDtypeStruct((2, ROWS, F),...  106 us

profile of v3, /device:TPU:2, one launch (start us, length us, event | category | flops | bytes accessed | tf_op | source)
XLA Modules:
  0.0 109.5 jit_solution(9179599225811918682)
XLA Ops:
  0.6 0.0 copy-start
  0.6 0.0 copy-start.1
  0.7 0.0 copy-start.2
  1.4 106.5 %shard_map.94 = f32[2,32,384]{2,1,0:T(8,128)} custom-call(s32[8,1,256]{2,1,0:T(1,128)} %rows_ref.1, s32[1,1]{1,0:T(1,128)S(6)} %copy.10.count_ref, bf16[1,512,2048]{2,1,0:T(8,128)(2,1)} %pool_hbm.1, bf16[1,1,256,384]{3,2,1,0:T(8,128)(2,1)} %targets_hbm.1, f32[1,2,32,384]{3,2,1,0:T(8,128)} %weights_ref.1), custom_call_target="tpu_custom_call" | custom-call | tf_op jit(solution)/shard_map/pallas_call | solution.py:512
  107.8 0.0 copy-done
  107.9 0.0 copy-done.1
  107.9 0.0 copy-done.2
  107.9 1.7 %fusion.5 = (f32[1,2,32,384]{3,2,1,0:T(8,128)}, f32[1,2,32,384]{3,2,1,0:T(8,128)}, f32[1,2,32,384]{3,2,1,0:T(8,128)}) fusion(f32[2,32,384]{2,1,0:T(8,128)} %shard_map.94, f32[1,2,32,384]{3,2,1,0:T(8,128)S(1)} %copy-done.1, f32[1,2,32,384]{3,2,1,0:T(8,128)S(1)} %copy-done.2, f32[1,2,32,384]{3,2,1,0:T(8,128)S(1)} %copy-done), kind=kLoop, calls=%fused_computation.9 | loop fusion | flops 368640 | bytes 688128 | tf_op jit(solution)/shard_map/broadcast_in_dim | solution.py:565
Async XLA Ops:
  0.6 107.2 %copy-start = (f32[1,2,32,384]{3,2,1,0:T(8,128)S(1)}, f32[1,2,32,384]{3,2,1,0:T(8,128)}, u32[]{:S(2)}) copy-start(f32[1,2,32,384]{3,2,1,0:T(8,128)} %weights_ref.1) | copy-start | bytes 294916
  0.6 107.2 %copy-start.1 = (f32[1,2,32,384]{3,2,1,0:T(8,128)S(1)}, f32[1,2,32,384]{3,2,1,0:T(8,128)}, u32[]{:S(2)}) copy-start(f32[1,2,32,384]{3,2,1,0:T(8,128)} %param.13) | copy-start | bytes 294916
  0.7 107.2 %copy-start.2 = (f32[1,2,32,384]{3,2,1,0:T(8,128)S(1)}, f32[1,2,32,384]{3,2,1,0:T(8,128)}, u32[]{:S(2)}) copy-start(f32[1,2,32,384]{3,2,1,0:T(8,128)} %param.12) | copy-start | bytes 294916
